TPU v7x, 32 devices: a whole 2x2x4 slice. The times are simulated.
32 devices in a mesh: row: 4 (over y, core), col: 8 (over z, x).
Axes of the slice: x: 2, y: 2, z: 4, core: 2. Of those that a mesh axis runs over, the one named last changes fastest.
Arguments:
- tokens: bfloat16 [3072, 6144], P('row'), may hold values from -6 to 6
- routes: int32 [3072, 2], P('row'), may hold values from 0 to 7, as said below
- w_master: float32 [6144, 2, 9216], P('row', None, 'col'), may hold values from -1 to 1
- d_hidden: bfloat16 [768, 9216], P('row', 'col'), may hold values from -6 to 6
Outputs:
- hidden: bfloat16 [768, 9216], P('row', 'col')
- update: float32 [6144, 2, 9216], P('row', None, 'col')
- new_master: float32 [6144, 2, 9216], P('row', None, 'col')
Inputs may be any that keep to these rules, and one draw needn't show every extreme that they name: `routes`: in every aligned block of 768 tokens exactly 192 tokens name expert 0; the two experts of a token differ; every expert is named.
All inputs are finite; a program needn't handle non-finite values. Where the computation divides by a largest or mean magnitude, that divisor is 1e-20 or more.
Results may differ from a plain program's by a relative error of at most 0.023.
Values may be sent and summed in bfloat16 or wider, within the bound.
A program may use at most 128 MiB of HBM per device.

v0:
```python
import jax
import jax.numpy as jnp
from jax import lax
from jax.sharding import PartitionSpec as P

BLK = 128


epsilon = 1e-06
quant_range = 448.0
learn_rate = 0.05


def on_device(tokens, routes, w_master, d_hidden):
    rows_local, _, columns = w_master.shape
    slots = d_hidden.shape[0]
    colmax = lax.pmax(jnp.max(jnp.abs(w_master), axis=0), "row")
    wscale = (colmax + epsilon) / quant_range
    quantized = (w_master / wscale).astype(jnp.bfloat16).reshape(rows_local, 2 * columns)
    flat_scale = wscale.reshape(2 * columns)
    routed = jnp.any(routes == 0, axis=1)
    picked = jnp.nonzero(routed, size=slots)[0].astype(jnp.int32)
    slot_rows = tokens[picked]
    slot_cols = lax.all_to_all(slot_rows, "row", split_axis=1, concat_axis=0, tiled=True)
    slot_part = lax.slice_in_dim(slot_cols, 0, lax.axis_size("row") * slots, axis=0)
    summed = lax.psum_scatter(
        jnp.dot(slot_part, quantized, preferred_element_type=jnp.float32).astype(jnp.bfloat16),
        "row",
        scatter_dimension=0,
        tiled=True,
    ).astype(jnp.float32)
    projected = (summed * flat_scale).reshape(slots, 2, columns)
    gate_pre = projected[:, 0]
    up_pre = projected[:, 1]
    gate_sig = jax.nn.sigmoid(gate_pre)
    gate_act = gate_pre * gate_sig
    hidden = (gate_act * up_pre).astype(jnp.bfloat16)
    upstream = d_hidden.astype(jnp.float32)
    grad_gate = upstream * up_pre * gate_sig * (1.0 + gate_pre * (1.0 - gate_sig))
    grad_up = upstream * gate_act
    grad_pre = (
        jnp.stack([grad_gate, grad_up], axis=1).astype(jnp.bfloat16).reshape(slots, 2 * columns)
    )
    shard_piece = lax.all_gather(grad_pre, "row", axis=0, tiled=True)
    groups = shard_piece.shape[0] // slots
    slot_part = lax.slice_in_dim(slot_cols, 0, shard_piece.shape[0], axis=0).reshape(
        groups, slots, rows_local
    )
    block_terms = jnp.einsum(
        "gsd,gsf->gdf",
        slot_part,
        shard_piece.reshape(groups, slots, 2 * columns),
        preferred_element_type=jnp.float32,
    )
    rounded = lax.optimization_barrier(block_terms.astype(jnp.bfloat16)).astype(jnp.float32)
    grad_full = jnp.sum(rounded, axis=0)
    grad_blocks = grad_full.reshape(rows_local // BLK, BLK, 2, columns)
    block_max = lax.pmax(jnp.max(jnp.abs(grad_blocks), axis=(1, 3)), "col")
    update = (grad_blocks / (block_max[:, None, :, None] + epsilon)).reshape(rows_local, 2, columns)
    new_master = w_master - learn_rate * colmax * update
    return (hidden, update, new_master)


def solution(mesh):
    in_specs = (P("row", None), P("row", None), P("row", None, "col"), P("row", "col"))
    out_specs = (P("row", "col"), P("row", None, "col"), P("row", None, "col"))
    return jax.shard_map(
        on_device, mesh=mesh, in_specs=in_specs, out_specs=out_specs, check_vma=False
    )
```

profile of v0, /device:TPU:0, one launch (start us, length us, event | category | flops | bytes accessed | tf_op | source)
XLA Modules:
  0.0 307.5 jit_solution(1906840966773680442)
XLA Ops:
  7.2 0.7 compare_reduce_fusion
  7.9 0.6 convert_reduce_fusion.1
  8.5 0.3 reduce-window.16
  8.8 0.1 slice.21
  8.9 0.1 slice_reduce_fusion
  9.0 0.1 add_bitcast_fusion
  9.1 5.8 %scatter_custom_fusion = s32[192]{0:T(256)S(1)} fusion(s32[768]{0:T(1024)S(1)} %fusion.8, s32[768]{0:T(1024)S(1)} %broadcast.51, s32[]{:T(128)} %constant.21.clone.1), kind=kCustom, calls=%fused_computation.43 | custom fusion | flops 768 | bytes 772 | tf_op jit(solution)/shard_map/scatter-add | solution.py:22
  15.0 0.3 reduce-window.24
  15.3 0.1 slice.23
  15.4 0.1 slice_reduce_fusion.1
  15.5 0.1 add_bitcast_fusion.1
  15.6 0.7 compare_select_fusion.1
  16.3 9.1 %gather_fusion = bf16[192,6144]{1,0:T(8,128)(2,1)S(1)} fusion(bf16[768,6144]{1,0:T(8,128)(2,1)} %param.4, s32[1024]{0:T(1024)S(1)} %pad_clamp_fusion), kind=kCustom, calls=%fused_computation | custom fusion | bytes 4719360 | tf_op jit(solution)/shard_map/gather | solution.py:23
  25.4 1.6 copy.39
  27.0 4.3 %all-to-all-start = ((bf16[192,4,1536]{2,0,1:T(8,128)(2,1)}), bf16[192,4,1536]{2,0,1:T(8,128)(2,1)S(1)}, u32[]{:S(2)}, u32[]{:S(2)}) async-start(bf16[192,4,1536]{2,0,1:T(8,128)(2,1)} %bitcast.57), calls=%async_computation | async-start | bytes 4718592 | tf_op jit(solution)/shard_map/all_to_all | solution.py:24
  31.3 0.0 reduce-scatter.2.cloned.1.call-start
  31.3 9.0 %abs_reduce_fusion = f32[2,1152]{1,0:T(2,128)S(1)} fusion(f32[1536,2,1152]{2,1,0:T(2,128)} %param.6), kind=kLoop, calls=%fused_computation.5 | loop fusion | flops 7075584 | bytes 14164992 | tf_op jit(solution)/shard_map/reduce_max | solution.py:17
  40.3 21.3 %pmax.14 = f32[2,1152]{1,0:T(2,128)S(1)} all-reduce(f32[2,1152]{1,0:T(2,128)S(1)} %abs_reduce_fusion), channel_id=1, replica_groups=mesh['row'=4,'col'=8] {'row'}, use_global_device_ids=true, to_apply=%region_8.9 | all-reduce | flops 2304 | bytes 18432 | tf_op jit(solution)/shard_map/pmax | solution.py:17
  61.7 6.6 %divide_convert_fusion = bf16[1536,2,1152]{2,1,0:T(2,128)(2,1)S(1)} fusion(f32[1536,2,1152]{2,1,0:T(2,128)} %param.6, f32[2,1152]{1,0:T(2,128)S(1)} %get-tuple-element.11), kind=kLoop, calls=%fused_computation.6 | loop fusion | flops 7077888 | bytes 21242880 | tf_op jit(solution)/shard_map/convert_element_type | solution.py:19
  68.3 4.3 %copy.18 = bf16[192,8,2,1152]{3,1,2,0:T(8,128)(2,1)} copy(bf16[192,8,2,1152]{3,2,1,0:T(2,128)(2,1)S(1)} %bitcast.55) | data formatting | bytes 14155776
  72.6 0.0 all-to-all-done
  72.6 10.0 %convolution_convert_fusion.1 = bf16[768,2304]{1,0:T(8,128)(2,1)} fusion(bf16[768,1536]{1,0:T(8,128)(2,1)S(1)} %bitcast.56, bf16[1536,2304]{1,0:T(8,128)(2,1)} %bitcast.59), kind=kOutput, calls=%fused_computation.8 | convolution fusion | flops 5437587456 | bytes 12976128 | tf_op jit(solution)/shard_map/dot_general | solution.py:27
  82.7 0.0 copy-start
  82.7 0.0 reduce-scatter.2.cloned.1.call-update
  82.7 0.0 all-gather.2.cloned.1.call-start
  82.7 42.6 %reduce-scatter.2.cloned.1.call-done = bf16[192,2304]{1,0:T(8,128)(2,1)} async-done(((bf16[768,2304]{1,0:T(8,128)(2,1)}), bf16[192,2304]{1,0:T(8,128)(2,1)}) %reduce-scatter.2.cloned.1.call-update) | async-done | bytes 884752 | tf_op jit(solution)/shard_map/reduce_scatter | solution.py:26
  125.4 2.5 convert_multiply_fusion
  127.9 3.1 %reshape.95 = f32[192,2,1152]{2,1,0:T(2,128)} reshape(f32[192,2304]{1,0:T(8,128)} %convert_multiply_fusion) | data formatting | bytes 3538944 | tf_op jit(solution)/shard_map/reshape | solution.py:32
  131.0 3.5 %fusion.11 = (f32[192,1,1152]{2,1,0:T(1,128)S(1)}, f32[192,1,1152]{2,1,0:T(1,128)S(1)}) fusion(f32[192,2,1152]{2,1,0:T(2,128)} %reshape.95), kind=kLoop, calls=%fused_computation.45 | loop fusion | bytes 3538944 | tf_op jit(solution)/shard_map/slice | solution.py:33
  134.5 0.0 copy-done
  134.5 1.3 fusion.7
  135.9 0.1 maximum_bitcast_fusion
  135.9 1.0 copy.16
  136.9 0.0 all-gather.2.cloned.1.call-update
  137.0 30.9 %all-gather.2.cloned.1.call-done = bf16[768,2304]{1,0:T(8,128)(2,1)} async-done(((bf16[192,2304]{1,0:T(8,128)(2,1)}), bf16[768,2304]{1,0:T(8,128)(2,1)}) %all-gather.2.cloned.1.call-update) | async-done | bytes 3538960 | tf_op jit(solution)/shard_map/all_gather | solution.py:44
  167.9 14.6 %convolution_convert_fusion = bf16[4,1536,2304]{2,1,0:T(8,128)(2,1)} fusion(bf16[4,192,2304]{2,1,0:T(8,128)(2,1)} %bitcast.60, bf16[192,4,1536]{2,0,1:T(8,128)(2,1)S(1)} %all-to-all-done), kind=kOutput, calls=%fused_computation.3 | convolution fusion | flops 5449973760 | bytes 34209792 | tf_op jit(solution)/shard_map/gsd,gsf->gdf/dot_general | solution.py:49
  182.5 22.4 %convert_reduce_fusion = f32[1536,2304]{1,0:T(8,128)} fusion(bf16[4,1536,2304]{2,1,0:T(8,128)(2,1)} %convolution_convert_fusion), kind=kLoop, calls=%fused_computation.2 | loop fusion | flops 24772608 | bytes 42467328 | tf_op jit(solution)/shard_map/reduce_sum | solution.py:56
  204.9 11.5 %abs.10 = f32[1536,2304]{1,0:T(8,128)} abs(f32[1536,2304]{1,0:T(8,128)} %convert_reduce_fusion) | non-fusion elementwise | flops 3538944 | bytes 28311552 | tf_op jit(solution)/shard_map/abs | solution.py:58
  216.4 17.2 %abs.11 = f32[12,128,2,1152]{3,2,1,0:T(2,128)} reshape(f32[1536,2304]{1,0:T(8,128)} %abs.10) | data formatting | bytes 28311552 | tf_op jit(solution)/shard_map/abs | solution.py:58
  233.7 8.0 %reduce_max.19 = f32[12,2]{1,0:T(8,128)S(1)} reduce(f32[12,128,2,1152]{3,2,1,0:T(2,128)} %abs.11, f32[]{:T(128)} %constant.48.clone.1), dimensions={1,3}, to_apply=%region_11.12 | reduce | flops 3538920 | bytes 14155876 | tf_op jit(solution)/shard_map/reduce_max | solution.py:58
  241.7 17.3 %reshape.97 = f32[1536,2,1152]{2,1,0:T(2,128)} reshape(f32[1536,2304]{1,0:T(8,128)} %convert_reduce_fusion) | data formatting | bytes 28311552 | tf_op jit(solution)/shard_map/reshape | solution.py:57
  259.0 21.6 %pmax.15 = f32[12,2]{1,0:T(8,128)S(1)} all-reduce(f32[12,2]{1,0:T(8,128)S(1)} %reduce_max.19), channel_id=1, replica_groups=mesh['row'=4,'col'=8] {'col'}, use_global_device_ids=true, to_apply=%region_12.13 | all-reduce | flops 24 | bytes 192 | tf_op jit(solution)/shard_map/pmax | solution.py:58
  280.6 0.1 div.42
  280.6 20.0 %multiply_subtract_fusion = (f32[1536,2,1152]{2,1,0:T(2,128)}, f32[1536,2,1152]{2,1,0:T(2,128)}) fusion(f32[1536,2,1152]{2,1,0:T(2,128)} %param.6, f32[2,1152]{1,0:T(2,128)S(1)} %get-tuple-element.10, f32[1536,2,1152]{2,1,0:T(2,128)} %reshape.97, f32[1536,2]{1,0:T(8,128)S(1)} %bitcast.62), kind=kLoop, calls=%fused_computation.4 | loop fusion | flops 10616832 | bytes 56644608 | tf_op jit(solution)/shard_map/sub | solution.py:60
  (10 shorter events, 0.1 us)
Async XLA Ops:
  27.0 45.6 %all-to-all-start = ((bf16[192,4,1536]{2,0,1:T(8,128)(2,1)}), bf16[192,4,1536]{2,0,1:T(8,128)(2,1)S(1)}, u32[]{:S(2)}, u32[]{:S(2)}) async-start(bf16[192,4,1536]{2,0,1:T(8,128)(2,1)} %bitcast.57), calls=%async_computation | async-start | bytes 4718592 | tf_op jit(solution)/shard_map/all_to_all | solution.py:24
  31.3 94.1 %reduce-scatter.2.cloned.1.call-start = ((), (), s32[]{:S(2)}) async-start(), calls=%async_computation.2 | async-start | bytes 4423680 | tf_op jit(solution)/shard_map/reduce_scatter | solution.py:26
  82.7 51.9 %copy-start = (bf16[192,1152]{1,0:T(8,128)(2,1)S(1)}, bf16[192,1152]{1,0:T(8,128)(2,1)}, u32[]{:S(2)}) copy-start(bf16[192,1152]{1,0:T(8,128)(2,1)} %param.7) | copy-start | bytes 1327108
  82.7 85.2 %all-gather.2.cloned.1.call-start = ((), (), s32[]{:S(2)}) async-start(), calls=%async_computation.3 | async-start | bytes 4423680 | tf_op jit(solution)/shard_map/all_gather | solution.py:44
Sparse Core Ops, SparseCore 0:
  82.8 42.5 reduce-scatter.1
  137.1 30.7 all-gather.1
where the time goes:
time: 309 us; the launch traced here: 308 us
  other arithmetic  90.3 us (29%)
  waiting for transfers between devices  73.6 us (24%)
  local copies, waits for them, and re-layouts  57.7 us (19%)
  blocking collectives  42.9 us (14%)
  matrix products  24.6 us (8%)
  between operations  14.2 us (5%)
  starting transfers between devices  4.31 us (1%)
    reduce_scatter x1, waiting for transfers between devices, on_device(): lax.psum_scatter(jnp.dot(slot_part, quantized, preferred_element_type=jnp...  42.6 us
    all_gather x1, waiting for transfers between devices, on_device(): shard_piece = lax.all_gather(grad_pre, 'row', axis=0, tiled=True)  30.9 us
    reduce_sum x1, other arithmetic, on_device(): grad_full = jnp.sum(rounded, axis=0)  22.4 us
    pmax x1, blocking collectives, on_device(): block_max = lax.pmax(jnp.max(jnp.abs(grad_blocks), axis=(1, 3)), 'col')  21.6 us
    pmax x1, blocking collectives, on_device(): colmax = lax.pmax(jnp.max(jnp.abs(w_master), axis=0), 'row')  21.3 us
    sub x1, other arithmetic, on_device(): new_master = w_master - learn_rate * colmax * update  20 us
    reshape x1, local copies, waits for them, and re-layouts, on_device(): grad_blocks = grad_full.reshape(rows_local // BLK, BLK, 2, columns)  17.3 us
    abs x1, local copies, waits for them, and re-layouts, on_device(): block_max = lax.pmax(jnp.max(jnp.abs(grad_blocks), axis=(1, 3)), 'col')  17.2 us
  transfers between devices with their start and end apart: 3, of which 2 were waited for; matrix products, arithmetic and copies ran while one was open for 6% of the time, Pallas kernels for 0%

commit v1 on v0

--- a/solution.py
+++ b/solution.py
@@ -1,6 +1,8 @@
 import jax
 import jax.numpy as jnp
 from jax import lax
+from jax.experimental import pallas as pl
+from jax.experimental.pallas import tpu as pltpu
 from jax.sharding import PartitionSpec as P
 
 BLK = 128
@@ -11,7 +13,7 @@
 learn_rate = 0.05
 
 
-def on_device(tokens, routes, w_master, d_hidden):
+def on_device_plain(tokens, routes, w_master, d_hidden):
     rows_local, _, columns = w_master.shape
     slots = d_hidden.shape[0]
     colmax = lax.pmax(jnp.max(jnp.abs(w_master), axis=0), "row")
@@ -61,6 +63,369 @@
     return (hidden, update, new_master)
 
 
+LANE = 128
+SUB = 8
+
+
+def moved(src, dst, send, recv, to):
+    return pltpu.make_async_remote_copy(
+        src_ref=src,
+        dst_ref=dst,
+        send_sem=send,
+        recv_sem=recv,
+        device_id={"row": to},
+        device_id_type=pl.DeviceIdType.MESH,
+    )
+
+
+def forward_kernel(
+    mask_ref, dh_ref, tok_hbm, w_hbm, hid_ref, sc_ref, ga_ref, cm_ref,
+    tokv, asend, wv, folded, cmx, psend, prec, keep, own, xsend, xrec,
+    tok_sem, w_sem, a_send, a_recv, c_send, c_recv, p_send, p_recv,
+    x_send, x_recv, ga_send, ga_recv, gp_send, gp_recv, gf_send, gf_recv,
+):
+    me = lax.axis_index("row")
+    core = lax.rem(me, 2)
+    partner = me + 1 - 2 * core
+    across = lax.rem(me + 2, 4)
+    diag = lax.rem(partner + 2, 4)
+    where_to = (me, across, partner, diag)
+    tiles = ga_ref.shape[0]
+    slots = hid_ref.shape[0]
+    rows = sc_ref.shape[1]
+    toks = mask_ref.shape[1]
+    chunks = w_sem.shape[1]
+    piece = rows // chunks
+
+    order = (3, 1, 2, 0)
+    tok_copies = {}
+    for j in order:
+        cols = pl.ds(pl.multiple_of(where_to[j] * rows, LANE), rows)
+        tok_copies[j] = pltpu.make_async_copy(tok_hbm.at[:, cols], tokv.at[j], tok_sem.at[j])
+        tok_copies[j].start()
+    w_copies = []
+    for k in range(chunks):
+        part = pl.ds(k * piece, piece)
+        for p in range(2):
+            w_copies.append(
+                pltpu.make_async_copy(w_hbm.at[part, p, :], wv.at[p, part], w_sem.at[p, k])
+            )
+            w_copies[-1].start()
+
+    barrier = pltpu.get_barrier_semaphore()
+    for j in (1, 2, 3):
+        pl.semaphore_signal(
+            barrier, inc=1, device_id={"row": where_to[j]}, device_id_type=pl.DeviceIdType.MESH
+        )
+
+    mask = mask_ref[...]
+    before = lax.broadcasted_iota(jnp.int32, (toks, toks), 0)
+    after = lax.broadcasted_iota(jnp.int32, (toks, toks), 1)
+    ladder = jnp.where(before < after, 1.0, 0.0).astype(jnp.bfloat16)
+    place = jnp.dot(mask, ladder, preferred_element_type=jnp.float32)[0:1, :].astype(jnp.int32)
+    flag = mask[0:1, :].astype(jnp.float32)
+    slot_id = lax.broadcasted_iota(jnp.int32, (slots, toks), 0)
+    pick = jnp.where(slot_id == place, flag, 0.0).astype(jnp.bfloat16)
+    pl.semaphore_wait(barrier, 3)
+
+    a_copies = {}
+    for j in order:
+        tok_copies[j].wait()
+        got = jnp.dot(pick, tokv[j], preferred_element_type=jnp.float32).astype(jnp.bfloat16)
+        if j == 0:
+            sc_ref[0:slots, :] = got
+        else:
+            asend[j - 1] = got
+            a_copies[j] = moved(
+                asend.at[j - 1],
+                sc_ref.at[pl.ds(j * slots, slots)],
+                a_send.at[j - 1],
+                a_recv.at[j - 1],
+                where_to[j],
+            )
+            a_copies[j].start()
+
+    folded[...] = jnp.zeros(folded.shape, jnp.float32)
+    for k in range(chunks):
+        for p in range(2):
+            w_copies[2 * k + p].wait()
+
+        def fold(t, carry, k=k):
+            cols = pl.ds(pl.multiple_of(t * LANE, LANE), LANE)
+            for p in range(2):
+                tile = jnp.abs(wv[p, k * piece : (k + 1) * piece, cols])
+                best = jnp.max(tile.reshape(-1, SUB, LANE), axis=0)
+                folded[p, :, cols] = jnp.maximum(folded[p, :, cols], best)
+            return carry
+
+        lax.fori_loop(0, tiles, fold, 0)
+    cmx[0] = jnp.zeros(cmx.shape[1:], jnp.float32)
+    for p in range(2):
+        cmx[0, p : p + 1, :] = jnp.max(folded[p], axis=0, keepdims=True)
+    c_copies = []
+    for j in (1, 2, 3):
+        c_copies.append(moved(cmx.at[0], cmx.at[j], c_send.at[j - 1], c_recv.at[j - 1], where_to[j]))
+        c_copies[-1].start()
+    for copy in c_copies:
+        copy.wait()
+    cm_ref[...] = jnp.maximum(jnp.maximum(cmx[0], cmx[1]), jnp.maximum(cmx[2], cmx[3]))
+    for j in (3, 1, 2):
+        a_copies[j].wait()
+
+    def scale_row(t, p):
+        cols = pl.ds(pl.multiple_of(t * LANE, LANE), LANE)
+        return (cm_ref[p : p + 1, cols] + epsilon) / quant_range
+
+    def swap(t):
+        return moved(psend.at[t], prec.at[t], p_send.at[t], p_recv.at[t], partner)
+
+    def cross(t):
+        return moved(xsend.at[t], xrec.at[t], x_send.at[t], x_recv.at[t], across)
+
+    def grad_block(t, j):
+        return ga_ref.at[t, pl.ds(j * slots, slots)]
+
+    def share_across(t):
+        return moved(grad_block(t, 0), grad_block(t, 1), ga_send.at[t], ga_recv.at[t], across)
+
+    def share_partner(t):
+        return moved(grad_block(t, 0), grad_block(t, 2), gp_send.at[t], gp_recv.at[t], partner)
+
+    def forward(t):
+        return moved(grad_block(t, 1), grad_block(t, 3), gf_send.at[t], gf_recv.at[t], partner)
+
+    def step(i, carry):
+        @pl.when(i < tiles)
+        def _():
+            t = i
+            halves = []
+            for p in range(2):
+                w = wv[p, :, pl.ds(pl.multiple_of(t * LANE, LANE), LANE)]
+                halves.append((w * (1.0 / scale_row(t, p))).astype(jnp.bfloat16))
+            quantized = jnp.concatenate(halves, axis=1)
+            term = jnp.dot(sc_ref[...], quantized, preferred_element_type=jnp.float32)
+            slot = lax.rem(t, 2)
+            psend[t] = term[2 * slots :].astype(jnp.bfloat16)
+            keep[slot] = term[: 2 * slots]
+            swap(t).start()
+
+        @pl.when(jnp.logical_and(i >= 1, i < tiles + 1))
+        def _():
+            t = i - 1
+            slot = lax.rem(t, 2)
+            swap(t).wait_recv()
+            own[slot] = keep[slot, :slots] + prec[t, :slots].astype(jnp.float32)
+            xsend[t] = (keep[slot, slots:] + prec[t, slots:].astype(jnp.float32)).astype(jnp.bfloat16)
+            cross(t).start()
+
+        @pl.when(jnp.logical_and(i >= 2, i < tiles + 2))
+        def _():
+            t = i - 2
+            cross(t).wait_recv()
+            total = own[lax.rem(t, 2)] + xrec[t].astype(jnp.float32)
+            gate_pre = total[:, :LANE] * scale_row(t, 0)
+            up_pre = total[:, LANE:] * scale_row(t, 1)
+            gate_sig = jax.nn.sigmoid(gate_pre)
+            gate_act = gate_pre * gate_sig
+            cols = pl.ds(pl.multiple_of(t * LANE, LANE), LANE)
+            hid_ref[:, cols] = (gate_act * up_pre).astype(jnp.bfloat16)
+            upstream = dh_ref[:, cols].astype(jnp.float32)
+            grad_gate = upstream * up_pre * gate_sig * (1.0 + gate_pre * (1.0 - gate_sig))
+            grad_up = upstream * gate_act
+            ga_ref[t, 0:slots, :] = jnp.concatenate([grad_gate, grad_up], axis=1).astype(jnp.bfloat16)
+            share_across(t).start()
+            share_partner(t).start()
+
+        @pl.when(i >= 3)
+        def _():
+            t = i - 3
+            share_across(t).wait_recv()
+            forward(t).start()
+
+        return carry
+
+    lax.fori_loop(0, tiles + 3, step, 0)
+
+    def finish(t, carry):
+        swap(t).wait_send()
+        cross(t).wait_send()
+        share_across(t).wait_send()
+        share_partner(t).wait()
+        forward(t).wait()
+        return carry
+
+    lax.fori_loop(0, tiles, finish, 0)
+
+
+def gradient_kernel(sc_ref, ga_ref, grad_ref, top_ref, turned):
+    tiles = ga_ref.shape[0]
+    depth = grad_ref.shape[0]
+    turned[...] = sc_ref[...].T
+    blocks = depth // BLK
+    tops = tuple(jnp.zeros((SUB, LANE), jnp.float32) for _ in range(2 * blocks))
+
+    def step(t, tops):
+        grad = jnp.dot(turned[...], ga_ref[t], preferred_element_type=jnp.float32)
+        grad_ref[:, pl.ds(pl.multiple_of(t * 2 * LANE, 2 * LANE), 2 * LANE)] = grad.astype(jnp.bfloat16)
+        out = []
+        for b in range(blocks):
+            for p in range(2):
+                tile = jnp.abs(grad[b * BLK : (b + 1) * BLK, p * LANE : (p + 1) * LANE])
+                out.append(jnp.maximum(tops[2 * b + p], jnp.max(tile.reshape(-1, SUB, LANE), axis=0)))
+        return tuple(out)
+
+    tops = lax.fori_loop(0, tiles, step, tops)
+    for n in range(2 * blocks):
+        top_ref[0, n] = tops[n]
+
+
+def update_kernel(inv_ref, cm_ref, w_hbm, grad_hbm, update_hbm, new_hbm, wv, uv, gv, w_sem, g_sem, u_sem, n_sem):
+    blocks = g_sem.shape[0]
+    columns = wv.shape[2]
+    tiles = columns // LANE
+
+    def part(b):
+        return pl.ds(pl.multiple_of(b * BLK, BLK), BLK)
+
+    def old(b, p):
+        return pltpu.make_async_copy(w_hbm.at[part(b), p, :], wv.at[p, part(b)], w_sem.at[p, b])
+
+    def gradient(b):
+        return pltpu.make_async_copy(grad_hbm.at[part(b)], gv.at[part(b)], g_sem.at[b])
+
+    def put_update(b, p):
+        return pltpu.make_async_copy(uv.at[p, part(b)], update_hbm.at[part(b), p, :], u_sem.at[p, b])
+
+    def put_new(b, p):
+        return pltpu.make_async_copy(wv.at[p, part(b)], new_hbm.at[part(b), p, :], n_sem.at[p, b])
+
+    def begin(b, carry):
+        gradient(b).start()
+        for p in range(2):
+            old(b, p).start()
+        return carry
+
+    def step(b, carry):
+        gradient(b).wait()
+        for p in range(2):
+            old(b, p).wait()
+            inverse = inv_ref[2 * b + p]
+            for t in range(tiles):
+                cols = slice(t * LANE, (t + 1) * LANE)
+                at = (2 * t + p) * LANE
+                update = gv[part(b), at : at + LANE].astype(jnp.float32) * inverse
+                uv[p, part(b), cols] = update
+                wv[p, part(b), cols] = wv[p, part(b), cols] - (learn_rate * cm_ref[p : p + 1, cols]) * update
+            put_update(b, p).start()
+            put_new(b, p).start()
+        return carry
+
+    def finish(b, carry):
+        for p in range(2):
+            put_update(b, p).wait()
+            put_new(b, p).wait()
+        return carry
+
+    lax.fori_loop(0, blocks, begin, 0)
+    lax.fori_loop(0, blocks, step, 0)
+    lax.fori_loop(0, blocks, finish, 0)
+
+
+def on_device(tokens, routes, w_master, d_hidden):
+    rows, _, columns = w_master.shape
+    slots = d_hidden.shape[0]
+    toks = tokens.shape[0]
+    depth = 3 * BLK
+    aligned = columns % LANE == 0 and rows % depth == 0 and slots % 16 == 0 and toks % LANE == 0
+    if lax.axis_size("row") != 4 or not aligned:
+        return on_device_plain(tokens, routes, w_master, d_hidden)
+    tiles = columns // LANE
+    bf16, f32 = jnp.bfloat16, jnp.float32
+    routed = jnp.any(routes == 0, axis=1).astype(bf16)
+    mask = jnp.broadcast_to(routed[None, :], (16, toks))
+    chunks = 6
+    blocks = rows // BLK
+    vmem = pl.BlockSpec(memory_space=pltpu.VMEM)
+    hbm = pl.BlockSpec(memory_space=pl.ANY)
+    dma = pltpu.SemaphoreType.DMA
+    wide = 2 * LANE
+    hidden, slot_cols, grads, colmax = pl.pallas_call(
+        forward_kernel,
+        name="forward_exchange",
+        out_shape=(
+            jax.ShapeDtypeStruct((slots, columns), bf16),
+            jax.ShapeDtypeStruct((4 * slots, rows), bf16),
+            jax.ShapeDtypeStruct((tiles, 4 * slots, wide), bf16),
+            jax.ShapeDtypeStruct((SUB, columns), f32),
+        ),
+        in_specs=[vmem, vmem, hbm, hbm],
+        out_specs=(vmem, vmem, vmem, vmem),
+        scratch_shapes=[
+            pltpu.VMEM((4, toks, rows), bf16),
+            pltpu.VMEM((3, slots, rows), bf16),
+            pltpu.VMEM((2, rows, columns), f32),
+            pltpu.VMEM((2, SUB, columns), f32),
+            pltpu.VMEM((4, SUB, columns), f32),
+            pltpu.VMEM((tiles, 2 * slots, wide), bf16),
+            pltpu.VMEM((tiles, 2 * slots, wide), bf16),
+            pltpu.VMEM((2, 2 * slots, wide), f32),
+            pltpu.VMEM((2, slots, wide), f32),
+            pltpu.VMEM((tiles, slots, wide), bf16),
+            pltpu.VMEM((tiles, slots, wide), bf16),
+            dma((4,)),
+            dma((2, chunks)),
+            dma((3,)),
+            dma((3,)),
+            dma((3,)),
+            dma((3,)),
+        ]
+        + [dma((tiles,))] * 10,
+        compiler_params=pltpu.CompilerParams(
+            collective_id=0, has_side_effects=True, vmem_limit_bytes=58 * 1024 * 1024
+        ),
+    )(mask, d_hidden, tokens, w_master)
+    steps = rows // depth
+    grad, tops = pl.pallas_call(
+        gradient_kernel,
+        name="weight_gradient",
+        grid=(steps,),
+        out_shape=(
+            jax.ShapeDtypeStruct((rows, 2 * columns), bf16),
+            jax.ShapeDtypeStruct((steps, 6, SUB, LANE), f32),
+        ),
+        in_specs=[
+            pl.BlockSpec((4 * slots, depth), lambda d: (0, d)),
+            pl.BlockSpec((tiles, 4 * slots, wide), lambda d: (0, 0, 0)),
+        ],
+        out_specs=(
+            pl.BlockSpec((depth, 2 * columns), lambda d: (d, 0)),
+            pl.BlockSpec((1, 6, SUB, LANE), lambda d: (d, 0, 0, 0)),
+        ),
+        scratch_shapes=[pltpu.VMEM((depth, 4 * slots), bf16)],
+        compiler_params=pltpu.CompilerParams(vmem_limit_bytes=32 * 1024 * 1024),
+    )(slot_cols, grads)
+    block_max = lax.pmax(jnp.max(tops, axis=(2, 3)).reshape(-1), "col")
+    inverse = 1.0 / (block_max + epsilon)
+    update, new_master = pl.pallas_call(
+        update_kernel,
+        name="master_update",
+        out_shape=(jax.ShapeDtypeStruct(w_master.shape, f32),) * 2,
+        in_specs=[pl.BlockSpec(memory_space=pltpu.SMEM), vmem, hbm, hbm],
+        out_specs=(hbm, hbm),
+        scratch_shapes=[
+            pltpu.VMEM((2, rows, columns), f32),
+            pltpu.VMEM((2, rows, columns), f32),
+            pltpu.VMEM((rows, 2 * columns), bf16),
+            dma((2, blocks)),
+            dma((blocks,)),
+            dma((2, blocks)),
+            dma((2, blocks)),
+        ],
+        compiler_params=pltpu.CompilerParams(vmem_limit_bytes=48 * 1024 * 1024),
+    )(inverse, colmax, w_master, grad)
+    return (hidden, update, new_master)
+
+
 def solution(mesh):
     in_specs = (P("row", None), P("row", None), P("row", None, "col"), P("row", "col"))
     out_specs = (P("row", "col"), P("row", None, "col"), P("row", None, "col"))

time: 309 us -> 144 us (0.47)
  Pallas kernels: 0 us -> 112 us
  other arithmetic: 90.3 us -> 0.85 us
  waiting for transfers between devices: 73.6 us -> 0 us
  local copies, waits for them, and re-layouts: 57.7 us -> 8.81 us
  matrix products: 24.6 us -> 0 us
  blocking collectives: 42.9 us -> 21.6 us
  between operations: 14.2 us -> 0.69 us
  starting transfers between devices: 4.31 us -> 0 us
    pallas_call x0 -> x3, Pallas kernels: none -> 112 us  [the longest x1 80.2 us: on_device(): pl.pallas_call(forward_kernel, name='forward_exchange', out_shape=(jax.Sh...]
    reduce_scatter x1 -> x0, waiting for transfers between devices: 42.6 us -> none  [on_device(): lax.psum_scatter(jnp.dot(slot_part, quantized, preferred_element_type=jnp...]
    all_gather x1 -> x0, waiting for transfers between devices: 30.9 us -> none  [on_device(): shard_piece = lax.all_gather(grad_pre, 'row', axis=0, tiled=True)]
    dot_general x2 -> x0, matrix products: 24.6 us -> none  [the longest x1 14.6 us: on_device(): jnp.einsum('gsd,gsf->gdf', slot_part, shard_piece.reshape(groups, slots,...]
    reduce_sum x2 -> x0, other arithmetic: 23.1 us -> none  [the longest x1 22.4 us: on_device(): grad_full = jnp.sum(rounded, axis=0)]
    pmax x2 -> x1, blocking collectives: 42.9 us -> 21.6 us  [on_device(): block_max = lax.pmax(jnp.max(tops, axis=(2, 3)).reshape(-1), 'col')]
    reshape x2 -> x1, local copies, waits for them, and re-layouts: 20.4 us -> 0.09 us  [on_device(): block_max = lax.pmax(jnp.max(tops, axis=(2, 3)).reshape(-1), 'col')]
    sub x1 -> x0, other arithmetic: 20 us -> none  [on_device(): new_master = w_master - learn_rate * colmax * update]
  transfers between devices with their start and end apart: 3 -> 0, of which waited for: 2 -> 0; matrix products, arithmetic and copies ran while one was open for 6% -> 0% of each run, Pallas kernels for 0% -> 0%
where the time goes in v1:
time: 144 us
  Pallas kernels  112 us (78%)
  blocking collectives  21.6 us (15%)
  local copies, waits for them, and re-layouts  8.81 us (6%)
    pallas_call x1, Pallas kernels, on_device(): pl.pallas_call(forward_kernel, name='forward_exchange', out_shape=(jax.Sh...  80.2 us
    pmax x1, blocking collectives, on_device(): block_max = lax.pmax(jnp.max(tops, axis=(2, 3)).reshape(-1), 'col')  21.6 us
    pallas_call x1, Pallas kernels, on_device(): pl.pallas_call(update_kernel, name='master_update', out_shape=(jax.ShapeD...  18.6 us
    pallas_call x1, Pallas kernels, on_device(): pl.pallas_call(gradient_kernel, name='weight_gradient', grid=(steps,), ou...  12.8 us
    unnamed x11, local copies, waits for them, and re-layouts  8.11 us

profile of v1, /device:TPU:0, one launch (start us, length us, event | category | flops | bytes accessed | tf_op | source)
XLA Modules:
  0.0 143.6 jit_solution(8268045746803520790)
XLA Ops:
  0.6 0.7 compare_reduce_fusion
  1.4 0.6 broadcast_in_dim.2.mask_ref
  2.0 80.2 %forward_exchange.1 = (bf16[192,1152]{1,0:T(8,128)(2,1)}, bf16[768,1536]{1,0:T(8,128)(2,1)}, bf16[9,768,256]{2,1,0:T(8,128)(2,1)}, f32[8,1152]{1,0:T(8,128)}) custom-call(bf16[16,768]{1,0:T(8,128)(2,1)} %broadcast_in_dim.2.mask_ref, bf16[192,1152]{1,0:T(8,128)(2,1)} %dh_ref.1, bf16[768,6144]{1,0:T(8,128)(2,1)} %tok_hbm.1, f32[1536,2,1152]{2,1,0:T(2,128)} %w_hbm.3), custom_call_target="tpu_custom_call" | custom-call | tf_op jit(solution)/shard_map/forward_exchange/pallas_call | solution.py:352
  82.2 0.0 copy-start.1
  82.2 2.0 %copy-done.1 = bf16[9,768,256]{2,1,0:T(8,128)(2,1)S(1)} copy-done((bf16[9,768,256]{2,1,0:T(8,128)(2,1)S(1)}, bf16[9,768,256]{2,1,0:T(8,128)(2,1)}, u32[]{:S(2)}) %copy-start.1) | copy-done | bytes 3538968
  84.2 0.0 copy-start.2
  84.2 1.7 %copy-done.2 = bf16[768,1536]{1,0:T(8,128)(2,1)S(1)} copy-done((bf16[768,1536]{1,0:T(8,128)(2,1)S(1)}, bf16[768,1536]{1,0:T(8,128)(2,1)}, u32[]{:S(2)}) %copy-start.2) | copy-done | bytes 2359320
  85.8 12.8 %weight_gradient.1 = (bf16[1536,2304]{1,0:T(8,128)(2,1)S(1)}, f32[4,6,8,128]{3,2,1,0:T(8,128)S(1)}) custom-call(bf16[768,1536]{1,0:T(8,128)(2,1)S(1)} %copy-done.2, bf16[9,768,256]{2,1,0:T(8,128)(2,1)S(1)} %copy-done.1), custom_call_target="tpu_custom_call" | custom-call | tf_op jit(solution)/shard_map/weight_gradient/pallas_call | solution.py:388
  98.7 0.0 copy-start
  98.7 2.9 %copy-done = bf16[1536,2304]{1,0:T(8,128)(2,1)} copy-done((bf16[1536,2304]{1,0:T(8,128)(2,1)}, bf16[1536,2304]{1,0:T(8,128)(2,1)S(1)}, u32[]{:S(2)}) %copy-start) | copy-done | bytes 7077912
  101.6 0.1 reduce_max.9
  101.7 0.1 reshape.12
  101.8 21.6 %pmax.7 = f32[24]{0:T(128)S(1)} all-reduce(f32[24]{0:T(128)S(1)} %reshape.12), channel_id=1, replica_groups=mesh['row'=4,'col'=8] {'col'}, use_global_device_ids=true, to_apply=%region_2.0 | all-reduce | flops 24 | bytes 192 | tf_op jit(solution)/shard_map/pmax | solution.py:407
  123.4 0.0 copy-start.3
  123.4 0.8 copy-done.3
  124.2 0.0 copy-start.4
  124.2 18.6 %master_update.1 = (f32[1536,2,1152]{2,1,0:T(2,128)}, f32[1536,2,1152]{2,1,0:T(2,128)}) custom-call(f32[24]{0:T(128)S(1)} %add_divide_fusion.inv_ref, f32[8,1152]{1,0:T(8,128)S(1)} %copy-done.3, f32[1536,2,1152]{2,1,0:T(2,128)} %w_hbm.3, bf16[1536,2304]{1,0:T(8,128)(2,1)} %copy-done), custom_call_target="tpu_custom_call" | custom-call | tf_op jit(solution)/shard_map/master_update/pallas_call | solution.py:409
  142.8 0.0 copy-done.4
  142.8 0.8 copy.8
  (2 shorter events, 0.0 us)
Async XLA Ops:
  82.2 2.0 %copy-start.1 = (bf16[9,768,256]{2,1,0:T(8,128)(2,1)S(1)}, bf16[9,768,256]{2,1,0:T(8,128)(2,1)}, u32[]{:S(2)}) copy-start(bf16[9,768,256]{2,1,0:T(8,128)(2,1)} %get-tuple-element.13.ga_ref) | copy-start | bytes 10616836
  84.2 1.7 %copy-start.2 = (bf16[768,1536]{1,0:T(8,128)(2,1)S(1)}, bf16[768,1536]{1,0:T(8,128)(2,1)}, u32[]{:S(2)}) copy-start(bf16[768,1536]{1,0:T(8,128)(2,1)} %get-tuple-element.12.sc_ref) | copy-start | bytes 7077892
  98.7 2.9 %copy-start = (bf16[1536,2304]{1,0:T(8,128)(2,1)}, bf16[1536,2304]{1,0:T(8,128)(2,1)S(1)}, u32[]{:S(2)}) copy-start(bf16[1536,2304]{1,0:T(8,128)(2,1)S(1)} %get-tuple-element.16.grad_hbm) | copy-start | bytes 21233668
  123.4 0.8 copy-start.3
  124.2 18.6 %copy-start.4 = (bf16[192,1152]{1,0:T(8,128)(2,1)S(1)}, bf16[192,1152]{1,0:T(8,128)(2,1)}, u32[]{:S(2)}) copy-start(bf16[192,1152]{1,0:T(8,128)(2,1)} %get-tuple-element.22) | copy-start | bytes 1327108

commit v2 on v1

--- a/solution.py
+++ b/solution.py
@@ -67,21 +67,21 @@
 SUB = 8
 
 
-def moved(src, dst, send, recv, to):
+def moved(src, dst, send, recv, to, axis="row"):
     return pltpu.make_async_remote_copy(
         src_ref=src,
         dst_ref=dst,
         send_sem=send,
         recv_sem=recv,
-        device_id={"row": to},
+        device_id={axis: to},
         device_id_type=pl.DeviceIdType.MESH,
     )
 
 
 def forward_kernel(
-    mask_ref, dh_ref, tok_hbm, w_hbm, hid_ref, sc_ref, ga_ref, cm_ref,
-    tokv, asend, wv, folded, cmx, psend, prec, keep, own, xsend, xrec,
-    tok_sem, w_sem, a_send, a_recv, c_send, c_recv, p_send, p_recv,
+    mask_ref, dh_ref, tok_hbm, w_hbm, hid_ref, grad_hbm, cm_ref, top_ref,
+    sc_ref, ga_ref, turned, gbuf, tops, topx, tokv, asend, hsend, wv, folded, cmx, psend, prec, keep, own, xsend, xrec,
+    tok_sem, w_sem, a_send, a_recv, y_send, y_recv, s_send, s_recv, t_send, t_recv, g_sem, c_send, c_recv, p_send, p_recv,
     x_send, x_recv, ga_send, ga_recv, gp_send, gp_recv, gf_send, gf_recv,
 ):
     me = lax.axis_index("row")
@@ -112,7 +112,19 @@
             )
             w_copies[-1].start()
 
+    col = lax.axis_index("col")
+    ncol = topx.shape[0]
+    side = lax.rem(col, 2)
+    beside = col + 1 - 2 * side
+    half = slots // 2
     barrier = pltpu.get_barrier_semaphore()
+    for d in range(1, ncol):
+        pl.semaphore_signal(
+            barrier,
+            inc=1,
+            device_id={"col": lax.rem(col + d, ncol)},
+            device_id_type=pl.DeviceIdType.MESH,
+        )
     for j in (1, 2, 3):
         pl.semaphore_signal(
             barrier, inc=1, device_id={"row": where_to[j]}, device_id_type=pl.DeviceIdType.MESH
@@ -126,24 +138,33 @@
     flag = mask[0:1, :].astype(jnp.float32)
     slot_id = lax.broadcasted_iota(jnp.int32, (slots, toks), 0)
     pick = jnp.where(slot_id == place, flag, 0.0).astype(jnp.bfloat16)
-    pl.semaphore_wait(barrier, 3)
-
-    a_copies = {}
-    for j in order:
+    half_id = lax.broadcasted_iota(jnp.int32, (half, toks), 0) + side * half
+    half_pick = jnp.where(half_id == place, flag, 0.0).astype(jnp.bfloat16)
+    pl.semaphore_wait(barrier, 3 + ncol - 1)
+
+    pieces = y_send.shape[1]
+    wide = rows // pieces
+
+    def segment(j, k):
+        lines = pl.ds(pl.multiple_of(j * slots + side * half, half), half)
+        return sc_ref.at[lines, k * wide : (k + 1) * wide]
+
+    far = []
+    for n, j in enumerate((3, 1)):
         tok_copies[j].wait()
-        got = jnp.dot(pick, tokv[j], preferred_element_type=jnp.float32).astype(jnp.bfloat16)
-        if j == 0:
-            sc_ref[0:slots, :] = got
-        else:
-            asend[j - 1] = got
-            a_copies[j] = moved(
-                asend.at[j - 1],
-                sc_ref.at[pl.ds(j * slots, slots)],
-                a_send.at[j - 1],
-                a_recv.at[j - 1],
-                where_to[j],
-            )
-            a_copies[j].start()
+        hsend[n] = jnp.dot(half_pick, tokv[j], preferred_element_type=jnp.float32).astype(jnp.bfloat16)
+        for k in range(pieces):
+            block = hsend.at[n, :, k * wide : (k + 1) * wide]
+            out = moved(block, segment(j, k), y_send.at[n, k], y_recv.at[n, k], where_to[j])
+            out.start()
+            on = moved(segment(j, k), segment(j, k), s_send.at[n, k], s_recv.at[n, k], beside, "col")
+            far.append((out, on))
+    tok_copies[2].wait()
+    asend[...] = jnp.dot(pick, tokv[2], preferred_element_type=jnp.float32).astype(jnp.bfloat16)
+    near = moved(asend, sc_ref.at[pl.ds(2 * slots, slots)], a_send, a_recv, partner)
+    near.start()
+    tok_copies[0].wait()
+    sc_ref[0:slots, :] = jnp.dot(pick, tokv[0], preferred_element_type=jnp.float32).astype(jnp.bfloat16)
 
     folded[...] = jnp.zeros(folded.shape, jnp.float32)
     for k in range(chunks):
@@ -159,6 +180,8 @@
             return carry
 
         lax.fori_loop(0, tiles, fold, 0)
+        far[k][0].wait_recv()
+        far[k][1].start()
     cmx[0] = jnp.zeros(cmx.shape[1:], jnp.float32)
     for p in range(2):
         cmx[0, p : p + 1, :] = jnp.max(folded[p], axis=0, keepdims=True)
@@ -166,11 +189,18 @@
     for j in (1, 2, 3):
         c_copies.append(moved(cmx.at[0], cmx.at[j], c_send.at[j - 1], c_recv.at[j - 1], where_to[j]))
         c_copies[-1].start()
+    for out, on in far[chunks:]:
+        out.wait_recv()
+        on.start()
     for copy in c_copies:
         copy.wait()
     cm_ref[...] = jnp.maximum(jnp.maximum(cmx[0], cmx[1]), jnp.maximum(cmx[2], cmx[3]))
-    for j in (3, 1, 2):
-        a_copies[j].wait()
+    near.wait()
+    for out, on in far:
+        out.wait_send()
+        on.wait()
+    tops[...] = jnp.zeros(tops.shape, jnp.float32)
+    blocks = tops.shape[0] // 2
 
     def scale_row(t, p):
         cols = pl.ds(pl.multiple_of(t * LANE, LANE), LANE)
@@ -193,6 +223,9 @@
 
     def forward(t):
         return moved(grad_block(t, 1), grad_block(t, 3), gf_send.at[t], gf_recv.at[t], partner)
+
+    def put_grad(t):
+        return pltpu.make_async_copy(gbuf.at[t], grad_hbm.at[t], g_sem.at[t])
 
     def step(i, carry):
         @pl.when(i < tiles)
@@ -236,47 +269,59 @@
             share_across(t).start()
             share_partner(t).start()
 
-        @pl.when(i >= 3)
+        @pl.when(jnp.logical_and(i >= 3, i < tiles + 3))
         def _():
             t = i - 3
             share_across(t).wait_recv()
             forward(t).start()
 
+        @pl.when(i < 4)
+        def _():
+            part = pl.ds(pl.multiple_of(i * (rows // 4), LANE), rows // 4)
+            turned[part, :] = sc_ref[:, part].T
+
+        @pl.when(i >= 4)
+        def _():
+            t = i - 4
+            share_partner(t).wait_recv()
+            forward(t).wait_recv()
+            grad = jnp.dot(turned[...], ga_ref[t], preferred_element_type=jnp.float32)
+            gbuf[t] = grad.astype(jnp.bfloat16)
+            for b in range(blocks):
+                for p in range(2):
+                    tile = jnp.abs(grad[b * BLK : (b + 1) * BLK, p * LANE : (p + 1) * LANE])
+                    best = jnp.max(tile.reshape(-1, SUB, LANE), axis=0)
+                    tops[2 * b + p] = jnp.maximum(tops[2 * b + p], best)
+            put_grad(t).start()
+
         return carry
 
-    lax.fori_loop(0, tiles + 3, step, 0)
+    lax.fori_loop(0, tiles + 4, step, 0)
+
+    topx[0] = jnp.max(tops[...], axis=1)
+    t_copies = []
+    for d in range(1, ncol):
+        t_copies.append(
+            moved(topx.at[0], topx.at[d], t_send.at[d], t_recv.at[d], lax.rem(col + d, ncol), "col")
+        )
+        t_copies[-1].start()
 
     def finish(t, carry):
         swap(t).wait_send()
         cross(t).wait_send()
         share_across(t).wait_send()
-        share_partner(t).wait()
-        forward(t).wait()
+        share_partner(t).wait_send()
+        forward(t).wait_send()
+        put_grad(t).wait()
         return carry
 
     lax.fori_loop(0, tiles, finish, 0)
-
-
-def gradient_kernel(sc_ref, ga_ref, grad_ref, top_ref, turned):
-    tiles = ga_ref.shape[0]
-    depth = grad_ref.shape[0]
-    turned[...] = sc_ref[...].T
-    blocks = depth // BLK
-    tops = tuple(jnp.zeros((SUB, LANE), jnp.float32) for _ in range(2 * blocks))
-
-    def step(t, tops):
-        grad = jnp.dot(turned[...], ga_ref[t], preferred_element_type=jnp.float32)
-        grad_ref[:, pl.ds(pl.multiple_of(t * 2 * LANE, 2 * LANE), 2 * LANE)] = grad.astype(jnp.bfloat16)
-        out = []
-        for b in range(blocks):
-            for p in range(2):
-                tile = jnp.abs(grad[b * BLK : (b + 1) * BLK, p * LANE : (p + 1) * LANE])
-                out.append(jnp.maximum(tops[2 * b + p], jnp.max(tile.reshape(-1, SUB, LANE), axis=0)))
-        return tuple(out)
-
-    tops = lax.fori_loop(0, tiles, step, tops)
-    for n in range(2 * blocks):
-        top_ref[0, n] = tops[n]
+    for copy in t_copies:
+        copy.wait()
+    top = topx[0]
+    for d in range(1, ncol):
+        top = jnp.maximum(top, topx[d])
+    top_ref[...] = jnp.broadcast_to(jnp.max(top, axis=1, keepdims=True), top_ref.shape)
 
 
 def update_kernel(inv_ref, cm_ref, w_hbm, grad_hbm, update_hbm, new_hbm, wv, uv, gv, w_sem, g_sem, u_sem, n_sem):
@@ -291,7 +336,7 @@
         return pltpu.make_async_copy(w_hbm.at[part(b), p, :], wv.at[p, part(b)], w_sem.at[p, b])
 
     def gradient(b):
-        return pltpu.make_async_copy(grad_hbm.at[part(b)], gv.at[part(b)], g_sem.at[b])
+        return pltpu.make_async_copy(grad_hbm.at[:, part(b)], gv.at[:, part(b)], g_sem.at[b])
 
     def put_update(b, p):
         return pltpu.make_async_copy(uv.at[p, part(b)], update_hbm.at[part(b), p, :], u_sem.at[p, b])
@@ -312,8 +357,7 @@
             inverse = inv_ref[2 * b + p]
             for t in range(tiles):
                 cols = slice(t * LANE, (t + 1) * LANE)
-                at = (2 * t + p) * LANE
-                update = gv[part(b), at : at + LANE].astype(jnp.float32) * inverse
+                update = gv[t, part(b), p * LANE : (p + 1) * LANE].astype(jnp.float32) * inverse
                 uv[p, part(b), cols] = update
                 wv[p, part(b), cols] = wv[p, part(b), cols] - (learn_rate * cm_ref[p : p + 1, cols]) * update
             put_update(b, p).start()
@@ -335,34 +379,42 @@
     rows, _, columns = w_master.shape
     slots = d_hidden.shape[0]
     toks = tokens.shape[0]
-    depth = 3 * BLK
-    aligned = columns % LANE == 0 and rows % depth == 0 and slots % 16 == 0 and toks % LANE == 0
-    if lax.axis_size("row") != 4 or not aligned:
+    ncol = lax.axis_size("col")
+    aligned = columns % LANE == 0 and rows % (4 * BLK) == 0 and slots % 32 == 0 and toks % LANE == 0
+    if lax.axis_size("row") != 4 or ncol % 2 or not aligned:
         return on_device_plain(tokens, routes, w_master, d_hidden)
     tiles = columns // LANE
     bf16, f32 = jnp.bfloat16, jnp.float32
     routed = jnp.any(routes == 0, axis=1).astype(bf16)
     mask = jnp.broadcast_to(routed[None, :], (16, toks))
-    chunks = 6
+    chunks = 4
+    pieces = 4
     blocks = rows // BLK
     vmem = pl.BlockSpec(memory_space=pltpu.VMEM)
     hbm = pl.BlockSpec(memory_space=pl.ANY)
     dma = pltpu.SemaphoreType.DMA
     wide = 2 * LANE
-    hidden, slot_cols, grads, colmax = pl.pallas_call(
+    hidden, grad, colmax, tops = pl.pallas_call(
         forward_kernel,
         name="forward_exchange",
         out_shape=(
             jax.ShapeDtypeStruct((slots, columns), bf16),
-            jax.ShapeDtypeStruct((4 * slots, rows), bf16),
-            jax.ShapeDtypeStruct((tiles, 4 * slots, wide), bf16),
+            jax.ShapeDtypeStruct((tiles, rows, wide), bf16),
             jax.ShapeDtypeStruct((SUB, columns), f32),
+            jax.ShapeDtypeStruct((2 * blocks, LANE), f32),
         ),
         in_specs=[vmem, vmem, hbm, hbm],
-        out_specs=(vmem, vmem, vmem, vmem),
+        out_specs=(vmem, hbm, vmem, vmem),
         scratch_shapes=[
+            pltpu.VMEM((4 * slots, rows), bf16),
+            pltpu.VMEM((tiles, 4 * slots, wide), bf16),
+            pltpu.VMEM((rows, 4 * slots), bf16),
+            pltpu.VMEM((tiles, rows, wide), bf16),
+            pltpu.VMEM((2 * blocks, SUB, LANE), f32),
+            pltpu.VMEM((ncol, 2 * blocks, LANE), f32),
             pltpu.VMEM((4, toks, rows), bf16),
-            pltpu.VMEM((3, slots, rows), bf16),
+            pltpu.VMEM((slots, rows), bf16),
+            pltpu.VMEM((2, slots // 2, rows), bf16),
             pltpu.VMEM((2, rows, columns), f32),
             pltpu.VMEM((2, SUB, columns), f32),
             pltpu.VMEM((4, SUB, columns), f32),
@@ -374,8 +426,15 @@
             pltpu.VMEM((tiles, slots, wide), bf16),
             dma((4,)),
             dma((2, chunks)),
-            dma((3,)),
-            dma((3,)),
+            dma,
+            dma,
+            dma((2, pieces)),
+            dma((2, pieces)),
+            dma((2, pieces)),
+            dma((2, pieces)),
+            dma((ncol,)),
+            dma((ncol,)),
+            dma((tiles,)),
             dma((3,)),
             dma((3,)),
         ]
@@ -384,28 +443,7 @@
             collective_id=0, has_side_effects=True, vmem_limit_bytes=58 * 1024 * 1024
         ),
     )(mask, d_hidden, tokens, w_master)
-    steps = rows // depth
-    grad, tops = pl.pallas_call(
-        gradient_kernel,
-        name="weight_gradient",
-        grid=(steps,),
-        out_shape=(
-            jax.ShapeDtypeStruct((rows, 2 * columns), bf16),
-            jax.ShapeDtypeStruct((steps, 6, SUB, LANE), f32),
-        ),
-        in_specs=[
-            pl.BlockSpec((4 * slots, depth), lambda d: (0, d)),
-            pl.BlockSpec((tiles, 4 * slots, wide), lambda d: (0, 0, 0)),
-        ],
-        out_specs=(
-            pl.BlockSpec((depth, 2 * columns), lambda d: (d, 0)),
-            pl.BlockSpec((1, 6, SUB, LANE), lambda d: (d, 0, 0, 0)),
-        ),
-        scratch_shapes=[pltpu.VMEM((depth, 4 * slots), bf16)],
-        compiler_params=pltpu.CompilerParams(vmem_limit_bytes=32 * 1024 * 1024),
-    )(slot_cols, grads)
-    block_max = lax.pmax(jnp.max(tops, axis=(2, 3)).reshape(-1), "col")
-    inverse = 1.0 / (block_max + epsilon)
+    inverse = 1.0 / (tops[:, 0] + epsilon)
     update, new_master = pl.pallas_call(
         update_kernel,
         name="master_update",
@@ -415,7 +453,7 @@
         scratch_shapes=[
             pltpu.VMEM((2, rows, columns), f32),
             pltpu.VMEM((2, rows, columns), f32),
-            pltpu.VMEM((rows, 2 * columns), bf16),
+            pltpu.VMEM((tiles, rows, wide), bf16),
             dma((2, blocks)),
             dma((blocks,)),
             dma((2, blocks)),

time: 144 us -> 99.2 us (0.69)
  blocking collectives: 21.6 us -> 0 us
  Pallas kernels: 112 us -> 94.6 us
  local copies, waits for them, and re-layouts: 8.81 us -> 2.15 us
    pmax x1 -> x0, blocking collectives: 21.6 us -> none  [on_device(): block_max = lax.pmax(jnp.max(tops, axis=(2, 3)).reshape(-1), 'col')]
    pallas_call x1 -> x0, Pallas kernels: 12.8 us -> none  [on_device(): pl.pallas_call(gradient_kernel, name='weight_gradient', grid=(steps,), ou...]
    unnamed x11 -> x5, local copies, waits for them, and re-layouts: 8.11 us -> 1.54 us
    pallas_call x1, Pallas kernels: 80.2 us -> 76 us  [on_device(): pl.pallas_call(forward_kernel, name='forward_exchange', out_shape=(jax.Sh...]
where the time goes in v2:
time: 99.2 us; the launch traced here: 98.9 us
  Pallas kernels  94.6 us (95%)
  local copies, waits for them, and re-layouts  2.15 us (2%)
  other arithmetic  1.54 us (2%)
    pallas_call x1, Pallas kernels, on_device(): pl.pallas_call(forward_kernel, name='forward_exchange', out_shape=(jax.Sh...  76 us
    pallas_call x1, Pallas kernels, on_device(): pl.pallas_call(update_kernel, name='master_update', out_shape=(jax.ShapeD...  18.6 us

profile of v2, /device:TPU:0, one launch (start us, length us, event | category | flops | bytes accessed | tf_op | source)
XLA Modules:
  0.0 98.9 jit_solution(7693446361091609779)
XLA Ops:
  0.6 0.7 compare_reduce_fusion
  1.4 0.6 broadcast_in_dim.2.mask_ref
  2.0 76.0 %forward_exchange.1 = (bf16[192,1152]{1,0:T(8,128)(2,1)}, bf16[9,1536,256]{2,1,0:T(8,128)(2,1)}, f32[8,1152]{1,0:T(8,128)}, f32[24,128]{1,0:T(8,128)}) custom-call(bf16[16,768]{1,0:T(8,128)(2,1)} %broadcast_in_dim.2.mask_ref, bf16[192,1152]{1,0:T(8,128)(2,1)} %dh_ref.1, bf16[768,6144]{1,0:T(8,128)(2,1)} %tok_hbm.1, f32[1536,2,1152]{2,1,0:T(2,128)} %w_hbm.3), custom_call_target="tpu_custom_call" | custom-call | tf_op jit(solution)/shard_map/forward_exchange/pallas_call | solution.py:397
  78.0 0.8 fusion.inv_ref
  78.8 0.0 copy-start
  78.8 0.8 copy-done
  79.6 0.0 copy-start.1
  79.6 18.6 %master_update.1 = (f32[1536,2,1152]{2,1,0:T(2,128)}, f32[1536,2,1152]{2,1,0:T(2,128)}) custom-call(f32[24]{0:T(128)S(1)} %fusion.inv_ref, f32[8,1152]{1,0:T(8,128)S(1)} %copy-done, f32[1536,2,1152]{2,1,0:T(2,128)} %w_hbm.3, bf16[9,1536,256]{2,1,0:T(8,128)(2,1)} %get-tuple-element.12.grad_hbm), custom_call_target="tpu_custom_call" | custom-call | tf_op jit(solution)/shard_map/master_update/pallas_call | solution.py:447
  98.2 0.0 copy-done.1
  98.2 0.8 copy.8
  (1 shorter events, 0.0 us)
Async XLA Ops:
  78.8 0.8 copy-start
  79.6 18.6 %copy-start.1 = (bf16[192,1152]{1,0:T(8,128)(2,1)S(1)}, bf16[192,1152]{1,0:T(8,128)(2,1)}, u32[]{:S(2)}) copy-start(bf16[192,1152]{1,0:T(8,128)(2,1)} %get-tuple-element.18) | copy-start | bytes 1327108

commit v3 on v2

--- a/solution.py
+++ b/solution.py
@@ -79,9 +79,9 @@
 
 
 def forward_kernel(
-    mask_ref, dh_ref, tok_hbm, w_hbm, hid_ref, grad_hbm, cm_ref, top_ref,
-    sc_ref, ga_ref, turned, gbuf, tops, topx, tokv, asend, hsend, wv, folded, cmx, psend, prec, keep, own, xsend, xrec,
-    tok_sem, w_sem, a_send, a_recv, y_send, y_recv, s_send, s_recv, t_send, t_recv, g_sem, c_send, c_recv, p_send, p_recv,
+    routes_ref, dh_ref, tok_hbm, w_hbm, hid_ref, gbuf, wv, cm_ref, top_ref,
+    sc_ref, ga_ref, turned, tops, topx, tokv, asend, hsend, folded, cmx, psend, prec, keep, own, xsend, xrec,
+    tok_sem, w_sem, a_send, a_recv, y_send, y_recv, s_send, s_recv, t_send, t_recv, c_send, c_recv, p_send, p_recv,
     x_send, x_recv, ga_send, ga_recv, gp_send, gp_recv, gf_send, gf_recv,
 ):
     me = lax.axis_index("row")
@@ -93,7 +93,7 @@
     tiles = ga_ref.shape[0]
     slots = hid_ref.shape[0]
     rows = sc_ref.shape[1]
-    toks = mask_ref.shape[1]
+    toks = routes_ref.shape[1]
     chunks = w_sem.shape[1]
     piece = rows // chunks
 
@@ -130,12 +130,13 @@
             barrier, inc=1, device_id={"row": where_to[j]}, device_id_type=pl.DeviceIdType.MESH
         )
 
-    mask = mask_ref[...]
+    named = jnp.logical_or(routes_ref[0:1, :] == 0, routes_ref[1:2, :] == 0)
+    flag = jnp.where(named, 1.0, 0.0)
+    mask = jnp.broadcast_to(flag, (16, toks)).astype(jnp.bfloat16)
     before = lax.broadcasted_iota(jnp.int32, (toks, toks), 0)
     after = lax.broadcasted_iota(jnp.int32, (toks, toks), 1)
     ladder = jnp.where(before < after, 1.0, 0.0).astype(jnp.bfloat16)
     place = jnp.dot(mask, ladder, preferred_element_type=jnp.float32)[0:1, :].astype(jnp.int32)
-    flag = mask[0:1, :].astype(jnp.float32)
     slot_id = lax.broadcasted_iota(jnp.int32, (slots, toks), 0)
     pick = jnp.where(slot_id == place, flag, 0.0).astype(jnp.bfloat16)
     half_id = lax.broadcasted_iota(jnp.int32, (half, toks), 0) + side * half
@@ -224,9 +225,6 @@
     def forward(t):
         return moved(grad_block(t, 1), grad_block(t, 3), gf_send.at[t], gf_recv.at[t], partner)
 
-    def put_grad(t):
-        return pltpu.make_async_copy(gbuf.at[t], grad_hbm.at[t], g_sem.at[t])
-
     def step(i, carry):
         @pl.when(i < tiles)
         def _():
@@ -292,7 +290,6 @@
                     tile = jnp.abs(grad[b * BLK : (b + 1) * BLK, p * LANE : (p + 1) * LANE])
                     best = jnp.max(tile.reshape(-1, SUB, LANE), axis=0)
                     tops[2 * b + p] = jnp.maximum(tops[2 * b + p], best)
-            put_grad(t).start()
 
         return carry
 
@@ -312,7 +309,6 @@
         share_across(t).wait_send()
         share_partner(t).wait_send()
         forward(t).wait_send()
-        put_grad(t).wait()
         return carry
 
     lax.fori_loop(0, tiles, finish, 0)
@@ -324,42 +320,27 @@
     top_ref[...] = jnp.broadcast_to(jnp.max(top, axis=1, keepdims=True), top_ref.shape)
 
 
-def update_kernel(inv_ref, cm_ref, w_hbm, grad_hbm, update_hbm, new_hbm, wv, uv, gv, w_sem, g_sem, u_sem, n_sem):
-    blocks = g_sem.shape[0]
-    columns = wv.shape[2]
-    tiles = columns // LANE
+def update_kernel(inv_ref, cm_ref, wv, gv, update_hbm, new_hbm, uv, nv, u_sem, n_sem):
+    blocks = u_sem.shape[1]
+    tiles = gv.shape[0]
 
     def part(b):
         return pl.ds(pl.multiple_of(b * BLK, BLK), BLK)
 
-    def old(b, p):
-        return pltpu.make_async_copy(w_hbm.at[part(b), p, :], wv.at[p, part(b)], w_sem.at[p, b])
-
-    def gradient(b):
-        return pltpu.make_async_copy(grad_hbm.at[:, part(b)], gv.at[:, part(b)], g_sem.at[b])
-
     def put_update(b, p):
         return pltpu.make_async_copy(uv.at[p, part(b)], update_hbm.at[part(b), p, :], u_sem.at[p, b])
 
     def put_new(b, p):
-        return pltpu.make_async_copy(wv.at[p, part(b)], new_hbm.at[part(b), p, :], n_sem.at[p, b])
-
-    def begin(b, carry):
-        gradient(b).start()
+        return pltpu.make_async_copy(nv.at[p, part(b)], new_hbm.at[part(b), p, :], n_sem.at[p, b])
+
+    def step(b, carry):
         for p in range(2):
-            old(b, p).start()
-        return carry
-
-    def step(b, carry):
-        gradient(b).wait()
-        for p in range(2):
-            old(b, p).wait()
             inverse = inv_ref[2 * b + p]
             for t in range(tiles):
                 cols = slice(t * LANE, (t + 1) * LANE)
                 update = gv[t, part(b), p * LANE : (p + 1) * LANE].astype(jnp.float32) * inverse
                 uv[p, part(b), cols] = update
-                wv[p, part(b), cols] = wv[p, part(b), cols] - (learn_rate * cm_ref[p : p + 1, cols]) * update
+                nv[p, part(b), cols] = wv[p, part(b), cols] - (learn_rate * cm_ref[p : p + 1, cols]) * update
             put_update(b, p).start()
             put_new(b, p).start()
         return carry
@@ -370,7 +351,6 @@
             put_new(b, p).wait()
         return carry
 
-    lax.fori_loop(0, blocks, begin, 0)
     lax.fori_loop(0, blocks, step, 0)
     lax.fori_loop(0, blocks, finish, 0)
 
@@ -385,8 +365,6 @@
         return on_device_plain(tokens, routes, w_master, d_hidden)
     tiles = columns // LANE
     bf16, f32 = jnp.bfloat16, jnp.float32
-    routed = jnp.any(routes == 0, axis=1).astype(bf16)
-    mask = jnp.broadcast_to(routed[None, :], (16, toks))
     chunks = 4
     pieces = 4
     blocks = rows // BLK
@@ -394,28 +372,27 @@
     hbm = pl.BlockSpec(memory_space=pl.ANY)
     dma = pltpu.SemaphoreType.DMA
     wide = 2 * LANE
-    hidden, grad, colmax, tops = pl.pallas_call(
+    hidden, grad, halves, colmax, tops = pl.pallas_call(
         forward_kernel,
         name="forward_exchange",
         out_shape=(
             jax.ShapeDtypeStruct((slots, columns), bf16),
-            jax.ShapeDtypeStruct((tiles, rows, wide), bf16),
+            pltpu.VMEM((tiles, rows, wide), bf16),
+            pltpu.VMEM((2, rows, columns), f32),
             jax.ShapeDtypeStruct((SUB, columns), f32),
             jax.ShapeDtypeStruct((2 * blocks, LANE), f32),
         ),
         in_specs=[vmem, vmem, hbm, hbm],
-        out_specs=(vmem, hbm, vmem, vmem),
+        out_specs=(vmem, vmem, vmem, vmem, vmem),
         scratch_shapes=[
             pltpu.VMEM((4 * slots, rows), bf16),
             pltpu.VMEM((tiles, 4 * slots, wide), bf16),
             pltpu.VMEM((rows, 4 * slots), bf16),
-            pltpu.VMEM((tiles, rows, wide), bf16),
             pltpu.VMEM((2 * blocks, SUB, LANE), f32),
             pltpu.VMEM((ncol, 2 * blocks, LANE), f32),
             pltpu.VMEM((4, toks, rows), bf16),
             pltpu.VMEM((slots, rows), bf16),
             pltpu.VMEM((2, slots // 2, rows), bf16),
-            pltpu.VMEM((2, rows, columns), f32),
             pltpu.VMEM((2, SUB, columns), f32),
             pltpu.VMEM((4, SUB, columns), f32),
             pltpu.VMEM((tiles, 2 * slots, wide), bf16),
@@ -434,33 +411,34 @@
             dma((2, pieces)),
             dma((ncol,)),
             dma((ncol,)),
-            dma((tiles,)),
             dma((3,)),
             dma((3,)),
         ]
         + [dma((tiles,))] * 10,
         compiler_params=pltpu.CompilerParams(
-            collective_id=0, has_side_effects=True, vmem_limit_bytes=58 * 1024 * 1024
+            collective_id=0, has_side_effects=True, vmem_limit_bytes=38 * 1024 * 1024
         ),
-    )(mask, d_hidden, tokens, w_master)
+    )(routes.T, d_hidden, tokens, w_master)
     inverse = 1.0 / (tops[:, 0] + epsilon)
     update, new_master = pl.pallas_call(
         update_kernel,
         name="master_update",
         out_shape=(jax.ShapeDtypeStruct(w_master.shape, f32),) * 2,
-        in_specs=[pl.BlockSpec(memory_space=pltpu.SMEM), vmem, hbm, hbm],
+        in_specs=[pl.BlockSpec(memory_space=pltpu.SMEM), vmem, vmem, vmem],
         out_specs=(hbm, hbm),
         scratch_shapes=[
             pltpu.VMEM((2, rows, columns), f32),
             pltpu.VMEM((2, rows, columns), f32),
-            pltpu.VMEM((tiles, rows, wide), bf16),
-            dma((2, blocks)),
-            dma((blocks,)),
             dma((2, blocks)),
             dma((2, blocks)),
         ],
-        compiler_params=pltpu.CompilerParams(vmem_limit_bytes=48 * 1024 * 1024),
-    )(inverse, colmax, w_master, grad)
+        compiler_params=pltpu.CompilerParams(vmem_limit_bytes=30 * 1024 * 1024),
+    )(
+        inverse,
+        colmax,
+        pltpu.with_memory_space_constraint(halves, pltpu.VMEM),
+        pltpu.with_memory_space_constraint(grad, pltpu.VMEM),
+    )
     return (hidden, update, new_master)
 
 

time: 99.2 us -> 89.6 us (0.903)
  Pallas kernels: 94.6 us -> 86.3 us
    pallas_call x1, Pallas kernels: 18.6 us -> 10.3 us  [on_device(): pl.pallas_call(update_kernel, name='master_update', out_shape=(jax.ShapeD...]
where the time goes in v3:
time: 89.6 us; the launch traced here: 89.3 us
  Pallas kernels  86.3 us (96%)
  local copies, waits for them, and re-layouts  1.54 us (2%)
    pallas_call x1, Pallas kernels, on_device(): pl.pallas_call(forward_kernel, name='forward_exchange', out_shape=(jax.Sh...  75.9 us
    pallas_call x1, Pallas kernels, on_device(): pl.pallas_call(update_kernel, name='master_update', out_shape=(jax.ShapeD...  10.3 us

profile of v3, /device:TPU:0, one launch (start us, length us, event | category | flops | bytes accessed | tf_op | source)
XLA Modules:
  0.0 89.3 jit_solution(7189517465564919759)
XLA Ops:
  0.6 75.9 %forward_exchange.1 = (bf16[192,1152]{1,0:T(8,128)(2,1)}, bf16[9,1536,256]{2,1,0:T(8,128)(2,1)S(1)}, f32[2,1536,1152]{2,1,0:T(8,128)S(1)}, f32[8,1152]{1,0:T(8,128)}, f32[24,128]{1,0:T(8,128)}) custom-call(s32[2,768]{1,0:T(2,128)} %bitcast.1, bf16[192,1152]{1,0:T(8,128)(2,1)} %dh_ref.1, bf16[768,6144]{1,0:T(8,128)(2,1)} %tok_hbm.1, f32[1536,2,1152]{2,1,0:T(2,128)} %w_hbm.1), custom_call_target="tpu_custom_call" | custom-call | tf_op jit(solution)/shard_map/forward_exchange/pallas_call | solution.py:375
  76.6 0.8 fusion.inv_ref
  77.4 0.0 copy-start
  77.4 0.8 copy-done
  78.2 0.0 copy-start.1
  78.2 10.3 %master_update.1 = (f32[1536,2,1152]{2,1,0:T(2,128)}, f32[1536,2,1152]{2,1,0:T(2,128)}) custom-call(f32[24]{0:T(128)S(1)} %fusion.inv_ref, f32[8,1152]{1,0:T(8,128)S(1)} %copy-done, f32[2,1536,1152]{2,1,0:T(8,128)S(1)} %get-tuple-element.13.wv, bf16[9,1536,256]{2,1,0:T(8,128)(2,1)S(1)} %get-tuple-element.14.gv), custom_call_target="tpu_custom_call" | custom-call | tf_op jit(solution)/shard_map/master_update/pallas_call | solution.py:423
  88.5 0.0 copy-done.1
  88.5 0.8 copy.8
Async XLA Ops:
  77.4 0.8 copy-start
  78.2 10.4 %copy-start.1 = (bf16[192,1152]{1,0:T(8,128)(2,1)S(1)}, bf16[192,1152]{1,0:T(8,128)(2,1)}, u32[]{:S(2)}) copy-start(bf16[192,1152]{1,0:T(8,128)(2,1)} %get-tuple-element.20) | copy-start | bytes 1327108

commit v4 on v3

--- a/solution.py
+++ b/solution.py
@@ -102,6 +102,7 @@
     for j in order:
         cols = pl.ds(pl.multiple_of(where_to[j] * rows, LANE), rows)
         tok_copies[j] = pltpu.make_async_copy(tok_hbm.at[:, cols], tokv.at[j], tok_sem.at[j])
+    for j in (3, 1):
         tok_copies[j].start()
     w_copies = []
     for k in range(chunks):
@@ -110,7 +111,6 @@
             w_copies.append(
                 pltpu.make_async_copy(w_hbm.at[part, p, :], wv.at[p, part], w_sem.at[p, k])
             )
-            w_copies[-1].start()
 
     col = lax.axis_index("col")
     ncol = topx.shape[0]
@@ -153,6 +153,9 @@
     far = []
     for n, j in enumerate((3, 1)):
         tok_copies[j].wait()
+        if n == 1:
+            for copy in (tok_copies[2], tok_copies[0], *w_copies):
+                copy.start()
         hsend[n] = jnp.dot(half_pick, tokv[j], preferred_element_type=jnp.float32).astype(jnp.bfloat16)
         for k in range(pieces):
             block = hsend.at[n, :, k * wide : (k + 1) * wide]

time: 89.6 us -> 90.1 us (level)
  no operation moved by 1% of the time
where the time goes in v4:
time: 90.1 us; the launch traced here: 89.8 us
  Pallas kernels  86.8 us (96%)
  local copies, waits for them, and re-layouts  1.54 us (2%)
    pallas_call x1, Pallas kernels, on_device(): pl.pallas_call(forward_kernel, name='forward_exchange', out_shape=(jax.Sh...  76.4 us
    pallas_call x1, Pallas kernels, on_device(): pl.pallas_call(update_kernel, name='master_update', out_shape=(jax.ShapeD...  10.3 us

profile of v4, /device:TPU:0, one launch (start us, length us, event | category | flops | bytes accessed | tf_op | source)
XLA Modules:
  0.0 89.8 jit_solution(10140218105361260566)
XLA Ops:
  0.6 76.4 %forward_exchange.1 = (bf16[192,1152]{1,0:T(8,128)(2,1)}, bf16[9,1536,256]{2,1,0:T(8,128)(2,1)S(1)}, f32[2,1536,1152]{2,1,0:T(8,128)S(1)}, f32[8,1152]{1,0:T(8,128)}, f32[24,128]{1,0:T(8,128)}) custom-call(s32[2,768]{1,0:T(2,128)} %bitcast.1, bf16[192,1152]{1,0:T(8,128)(2,1)} %dh_ref.1, bf16[768,6144]{1,0:T(8,128)(2,1)} %tok_hbm.1, f32[1536,2,1152]{2,1,0:T(2,128)} %w_hbm.1), custom_call_target="tpu_custom_call" | custom-call | tf_op jit(solution)/shard_map/forward_exchange/pallas_call | solution.py:378
  77.0 0.8 fusion.inv_ref
  77.9 0.0 copy-start
  77.9 0.8 copy-done
  78.6 0.0 copy-start.1
  78.7 10.3 %master_update.1 = (f32[1536,2,1152]{2,1,0:T(2,128)}, f32[1536,2,1152]{2,1,0:T(2,128)}) custom-call(f32[24]{0:T(128)S(1)} %fusion.inv_ref, f32[8,1152]{1,0:T(8,128)S(1)} %copy-done, f32[2,1536,1152]{2,1,0:T(8,128)S(1)} %get-tuple-element.13.wv, bf16[9,1536,256]{2,1,0:T(8,128)(2,1)S(1)} %get-tuple-element.14.gv), custom_call_target="tpu_custom_call" | custom-call | tf_op jit(solution)/shard_map/master_update/pallas_call | solution.py:426
  89.0 0.0 copy-done.1
  89.0 0.8 copy.8
Async XLA Ops:
  77.9 0.8 copy-start
  78.6 10.4 %copy-start.1 = (bf16[192,1152]{1,0:T(8,128)(2,1)S(1)}, bf16[192,1152]{1,0:T(8,128)(2,1)}, u32[]{:S(2)}) copy-start(bf16[192,1152]{1,0:T(8,128)(2,1)} %get-tuple-element.20) | copy-start | bytes 1327108
